TPU v7x, 32 devices: a whole 2x2x4 slice. The times are simulated.
32 devices in a mesh: dp: 4 (over y, core), tensor: 8 (over z, x).
Axes of the slice: x: 2, y: 2, z: 4, core: 2. Of those that a mesh axis runs over, the one named last changes fastest.
Arguments:
- block_input: float32 [4, 2048, 1024], P('dp', 'tensor'), may hold values from -6 to 6
- segment_ids: int32 [4, 2048], P('dp'), may hold values from 0 to 2, as said below
- positions: int32 [4, 2048], P('dp'), may hold values from 0 to 1791, as said below
- attention_gain: bfloat16 [1024], P('dp'), may hold values from 0.099609375 to 1.8984375
- feedforward_gain: bfloat16 [1024], P('dp'), may hold values from 0.099609375 to 1.8984375
- qkv_weight: bfloat16 [1024, 3, 1024], P('dp', None, 'tensor'), may hold values from -2 to 2, as said below
- output_weight: bfloat16 [1024, 1024], P('tensor', 'dp'), may hold values from -0.75 to 0.75
- expand_weight: bfloat16 [1024, 2, 2624], P('dp', None, 'tensor'), may hold values from -0.1875 to 0.1875
- contract_weight: bfloat16 [2624, 1024], P('tensor', 'dp'), may hold values from -0.25 to 0.25
- cotangent: float32 [4, 2048, 1024], P('dp', 'tensor'), may hold values from -6 to 6
Outputs:
- block_output: float32 [4, 2048, 1024], P('dp', 'tensor')
- input_grad: float32 [4, 2048, 1024], P('dp', 'tensor')
- attention_gain_grad: float32 [1024], P('dp')
- feedforward_gain_grad: float32 [1024], P('dp')
- qkv_grad: float32 [1024, 3, 1024], P('dp', None, 'tensor')
- output_grad: float32 [1024, 1024], P('tensor', 'dp')
- expand_grad: float32 [1024, 2, 2624], P('dp', None, 'tensor')
- contract_grad: float32 [2624, 1024], P('tensor', 'dp')
Inputs may be any that keep to these rules, and one draw needn't show every extreme that they name: `segment_ids`: within each sequence the numbers never fall; a token's number tells its document, and a number may be skipped. `positions`: each token's position counts the tokens before it in its own document; no document is longer than 1792 tokens, and some document is that long. `qkv_weight`: the joined query, key and value projection.
All inputs are finite; a program needn't handle non-finite values.
Results may differ from a plain program's by a relative error of at most 0.025.
Values may be sent and summed in bfloat16 or wider, within the bound.
A program may use at most 128 MiB of HBM per device.

v0:
```python
import math
import jax
import jax.numpy as jnp
from jax import lax
from jax.sharding import PartitionSpec as P

HD = 64
WINDOW = 128
EPSILON = 1e-05
MASKED = -1e30
ROOT_HALF = 0.7071067811865476
DENSITY = 0.3989422804014327


def layer_norm(values, gain_vector):
    centre = values - jnp.mean(values, axis=-1, keepdims=True)
    variance = jnp.mean(centre * centre, axis=-1, keepdims=True)
    inverse = lax.rsqrt(variance + EPSILON)
    normed = centre * inverse
    return (normed, inverse, (normed * gain_vector.astype(jnp.float32)).astype(jnp.bfloat16))


def norm_backward(upstream, normed, inverse, gain_vector):
    scaled = upstream * gain_vector.astype(jnp.float32)
    inner_term = (
        scaled
        - jnp.mean(scaled, axis=-1, keepdims=True)
        - normed * jnp.mean(scaled * normed, axis=-1, keepdims=True)
    )
    return (inverse * inner_term, jnp.sum(upstream * normed, axis=0))


def gelu_pair(values):
    normal_cdf = 0.5 * (1.0 + lax.erf(values * ROOT_HALF))
    return (values * normal_cdf, normal_cdf + values * DENSITY * jnp.exp(-0.5 * values * values))


def rope_tables(places, head_size):
    half_size = head_size // 2
    frequency = jnp.exp(
        jnp.arange(half_size, dtype=jnp.float32) * (-2.0 * math.log(10000.0) / head_size)
    )
    angles = places.astype(jnp.float32)[:, None] * frequency[None, :]
    cosine_table = jnp.concatenate([jnp.cos(angles), jnp.cos(angles)], axis=-1)[:, None, :]
    sine_table = jnp.concatenate([jnp.sin(angles), jnp.sin(angles)], axis=-1)[:, None, :]
    return (cosine_table, sine_table)


def rotate(tensor, cosine_table, sine_table):
    half_size = tensor.shape[-1] // 2
    turned = jnp.concatenate([-tensor[..., half_size:], tensor[..., :half_size]], axis=-1)
    return tensor * cosine_table + turned * sine_table


def unrotate(tensor, cosine_table, sine_table):
    half_size = tensor.shape[-1] // 2
    weighted = tensor * sine_table
    turned = jnp.concatenate([weighted[..., half_size:], -weighted[..., :half_size]], axis=-1)
    return tensor * cosine_table + turned


def block_scores(query_block, key_block, segment_query, segment_key, block_rows, scale):
    reach = WINDOW // 2
    scores = (
        jnp.einsum("qhd,khd->hqk", query_block, key_block, preferred_element_type=jnp.float32)
        * scale
    )
    offset = jnp.arange(block_rows)[:, None] + reach - jnp.arange(block_rows + 2 * reach)[None, :]
    valid = (jnp.abs(offset) <= reach) & (segment_query[:, None] == segment_key[None, :])
    return jnp.where(valid[None], scores, MASKED)


def band_pads(keys, values, segments):
    reach = WINDOW // 2
    pad_keys = jnp.pad(keys, ((reach, reach), (0, 0), (0, 0)))
    pad_values = jnp.pad(values, ((reach, reach), (0, 0), (0, 0)))
    pad_segments = jnp.pad(segments, (reach, reach), constant_values=-1)
    return (pad_keys, pad_values, pad_segments)


def band_forward(queries, keys, values, segments):
    length, heads, head_size = queries.shape
    reach = WINDOW // 2
    block = min(length, 512)
    scale = head_size ** (-0.5)
    pad_keys, pad_values, pad_segments = band_pads(keys, values, segments)

    def one_block(index):
        start = index * block
        query_block = lax.dynamic_slice_in_dim(queries, start, block, 0)
        key_block = lax.dynamic_slice_in_dim(pad_keys, start, block + 2 * reach, 0)
        value_block = lax.dynamic_slice_in_dim(pad_values, start, block + 2 * reach, 0)
        segment_query = lax.dynamic_slice_in_dim(segments, start, block, 0)
        segment_key = lax.dynamic_slice_in_dim(pad_segments, start, block + 2 * reach, 0)
        scores = block_scores(query_block, key_block, segment_query, segment_key, block, scale)
        peak = jnp.max(scores, axis=-1, keepdims=True)
        log_total = peak + jnp.log(jnp.sum(jnp.exp(scores - peak), axis=-1, keepdims=True))
        weights = jnp.exp(scores - log_total).astype(jnp.bfloat16)
        context = jnp.einsum(
            "hqk,khd->qhd", weights, value_block, preferred_element_type=jnp.float32
        ).astype(jnp.bfloat16)
        return (context, log_total[..., 0])

    contexts, totals = lax.map(one_block, jnp.arange(length // block, dtype=jnp.int32))
    return (contexts.reshape(length, heads, head_size), totals)


def band_backward(queries, keys, values, segments, grad_context, totals):
    length, heads, head_size = queries.shape
    reach = WINDOW // 2
    block = min(length, 512)
    span = block + 2 * reach
    scale = head_size ** (-0.5)
    pad_keys, pad_values, pad_segments = band_pads(keys, values, segments)

    def one_block(carry, index):
        grad_keys, grad_values = carry
        start = index * block
        query_block = lax.dynamic_slice_in_dim(queries, start, block, 0)
        key_block = lax.dynamic_slice_in_dim(pad_keys, start, span, 0)
        value_block = lax.dynamic_slice_in_dim(pad_values, start, span, 0)
        segment_query = lax.dynamic_slice_in_dim(segments, start, block, 0)
        segment_key = lax.dynamic_slice_in_dim(pad_segments, start, span, 0)
        grad_block = lax.dynamic_slice_in_dim(grad_context, start, block, 0)
        scores = block_scores(query_block, key_block, segment_query, segment_key, block, scale)
        probs = jnp.exp(scores - totals[index][..., None])
        grad_probs = jnp.einsum(
            "qhd,khd->hqk", grad_block, value_block, preferred_element_type=jnp.float32
        )
        delta = jnp.sum(probs * grad_probs, axis=-1, keepdims=True)
        grad_scores = (probs * (grad_probs - delta) * scale).astype(jnp.bfloat16)
        grad_query = jnp.einsum(
            "hqk,khd->qhd", grad_scores, key_block, preferred_element_type=jnp.float32
        )
        key_part = jnp.einsum(
            "hqk,qhd->khd", grad_scores, query_block, preferred_element_type=jnp.float32
        )
        value_part = jnp.einsum(
            "hqk,qhd->khd",
            probs.astype(jnp.bfloat16),
            grad_block,
            preferred_element_type=jnp.float32,
        )
        grad_keys = lax.dynamic_update_slice_in_dim(
            grad_keys, lax.dynamic_slice_in_dim(grad_keys, start, span, 0) + key_part, start, 0
        )
        grad_values = lax.dynamic_update_slice_in_dim(
            grad_values,
            lax.dynamic_slice_in_dim(grad_values, start, span, 0) + value_part,
            start,
            0,
        )
        return ((grad_keys, grad_values), grad_query)

    zeros = jnp.zeros((length + 2 * reach, heads, head_size), jnp.float32)
    (grad_keys, grad_values), grad_queries = lax.scan(
        one_block, (zeros, zeros), jnp.arange(length // block, dtype=jnp.int32)
    )
    return (
        grad_queries.reshape(length, heads, head_size),
        grad_keys[reach : reach + length],
        grad_values[reach : reach + length],
    )


def body(
    block_input,
    segment_ids,
    positions,
    attention_gain,
    feedforward_gain,
    qkv_weight,
    output_weight,
    expand_weight,
    contract_weight,
    cotangent,
):
    batches, local_rows, width = block_input.shape
    head_width = qkv_weight.shape[2]
    heads_here = head_width // HD
    unit_count = expand_weight.shape[2]
    qkv_full, expand_full, output_full, contract_full, first_gain, second_gain = (
        lax.all_gather(qkv_weight, "dp", axis=0, tiled=True),
        lax.all_gather(expand_weight, "dp", axis=0, tiled=True),
        lax.all_gather(output_weight, "dp", axis=1, tiled=True),
        lax.all_gather(contract_weight, "dp", axis=1, tiled=True),
        lax.all_gather(attention_gain, "dp", axis=0, tiled=True),
        lax.all_gather(feedforward_gain, "dp", axis=0, tiled=True),
    )
    qkv_matrix = qkv_full.reshape(width, 3 * head_width)
    expand_matrix = expand_full.reshape(width, 2 * unit_count)
    tokens = block_input[0]
    segments = segment_ids[0]
    cosine_table, sine_table = rope_tables(positions[0], HD)
    normed_one, inverse_one, rounded_one = layer_norm(tokens, first_gain)
    rows_one = lax.all_gather(rounded_one, "tensor", axis=0, tiled=True)
    length_all = rows_one.shape[0]
    projected = jnp.dot(rows_one, qkv_matrix, preferred_element_type=jnp.float32).reshape(
        length_all, 3, heads_here, HD
    )
    queries = rotate(projected[:, 0], cosine_table, sine_table).astype(jnp.bfloat16)
    keys = rotate(projected[:, 1], cosine_table, sine_table).astype(jnp.bfloat16)
    values_in = projected[:, 2].astype(jnp.bfloat16)
    context, totals = band_forward(queries, keys, values_in, segments)
    context_rows = context.reshape(length_all, head_width)
    attended = lax.psum_scatter(
        jnp.dot(context_rows, output_full, preferred_element_type=jnp.float32).astype(jnp.bfloat16),
        "tensor",
        scatter_dimension=0,
        tiled=True,
    ).astype(jnp.float32)
    residual = tokens + attended
    normed_two, inverse_two, rounded_two = layer_norm(residual, second_gain)
    rows_two = lax.all_gather(rounded_two, "tensor", axis=0, tiled=True)
    expanded = jnp.dot(rows_two, expand_matrix, preferred_element_type=jnp.float32).reshape(
        length_all, 2, unit_count
    )
    activated, slope = gelu_pair(expanded[:, 0])
    hidden = (activated * expanded[:, 1]).astype(jnp.bfloat16)
    contracted = lax.psum_scatter(
        jnp.dot(hidden, contract_full, preferred_element_type=jnp.float32).astype(jnp.bfloat16),
        "tensor",
        scatter_dimension=0,
        tiled=True,
    ).astype(jnp.float32)
    results = [residual + contracted]
    upstream = cotangent[0]
    rows_back = lax.all_gather(upstream.astype(jnp.bfloat16), "tensor", axis=0, tiled=True)
    grad_contract = jnp.dot(hidden.T, rows_back, preferred_element_type=jnp.float32)
    grad_hidden = jnp.dot(rows_back, contract_full.T, preferred_element_type=jnp.float32)
    grad_units = (
        jnp.stack([grad_hidden * expanded[:, 1] * slope, grad_hidden * activated], axis=1)
        .astype(jnp.bfloat16)
        .reshape(length_all, 2 * unit_count)
    )
    grad_expand = jnp.dot(rows_two.T, grad_units, preferred_element_type=jnp.float32)
    grad_two = lax.psum_scatter(
        jnp.dot(grad_units, expand_matrix.T, preferred_element_type=jnp.float32).astype(
            jnp.bfloat16
        ),
        "tensor",
        scatter_dimension=0,
        tiled=True,
    ).astype(jnp.float32)
    through_two, gain_part = norm_backward(grad_two, normed_two, inverse_two, second_gain)
    gain_second = gain_part
    grad_mid = upstream + through_two
    rows_mid = lax.all_gather(grad_mid.astype(jnp.bfloat16), "tensor", axis=0, tiled=True)
    grad_output = jnp.dot(context_rows.T, rows_mid, preferred_element_type=jnp.float32)
    grad_context = (
        jnp.dot(rows_mid, output_full.T, preferred_element_type=jnp.float32)
        .astype(jnp.bfloat16)
        .reshape(length_all, heads_here, HD)
    )
    grad_queries, grad_keys, grad_values = band_backward(
        queries, keys, values_in, segments, grad_context, totals
    )
    grad_proj = (
        jnp.stack(
            [
                unrotate(grad_queries, cosine_table, sine_table),
                unrotate(grad_keys, cosine_table, sine_table),
                grad_values,
            ],
            axis=1,
        )
        .astype(jnp.bfloat16)
        .reshape(length_all, 3 * head_width)
    )
    grad_qkv = jnp.dot(rows_one.T, grad_proj, preferred_element_type=jnp.float32)
    grad_one = lax.psum_scatter(
        jnp.dot(grad_proj, qkv_matrix.T, preferred_element_type=jnp.float32).astype(jnp.bfloat16),
        "tensor",
        scatter_dimension=0,
        tiled=True,
    ).astype(jnp.float32)
    through_one, gain_part = norm_backward(grad_one, normed_one, inverse_one, first_gain)
    input_grads = [grad_mid + through_one]
    gains_local = jnp.stack([gain_part, gain_second])
    owned_qkv, owned_expand, owned_output, owned_contract, owned_gains = (
        lax.psum_scatter(
            grad_qkv.reshape(width, 3, head_width).astype(jnp.bfloat16),
            "dp",
            scatter_dimension=0,
            tiled=True,
        ).astype(jnp.float32),
        lax.psum_scatter(
            grad_expand.reshape(width, 2, unit_count).astype(jnp.bfloat16),
            "dp",
            scatter_dimension=0,
            tiled=True,
        ).astype(jnp.float32),
        lax.psum_scatter(
            grad_output.astype(jnp.bfloat16), "dp", scatter_dimension=1, tiled=True
        ).astype(jnp.float32),
        lax.psum_scatter(
            grad_contract.astype(jnp.bfloat16), "dp", scatter_dimension=1, tiled=True
        ).astype(jnp.float32),
        lax.psum_scatter(
            gains_local.astype(jnp.bfloat16), "dp", scatter_dimension=1, tiled=True
        ).astype(jnp.float32),
    )
    gains_total = lax.psum(owned_gains, "tensor")
    return (
        jnp.stack(results),
        jnp.stack(input_grads),
        gains_total[0],
        gains_total[1],
        owned_qkv,
        owned_output,
        owned_expand,
        owned_contract,
    )


def solution(mesh):
    return jax.shard_map(
        body,
        mesh=mesh,
        in_specs=(
            P("dp", "tensor", None),
            P("dp", None),
            P("dp", None),
            P("dp"),
            P("dp"),
            P("dp", None, "tensor"),
            P("tensor", "dp"),
            P("dp", None, "tensor"),
            P("tensor", "dp"),
            P("dp", "tensor", None),
        ),
        out_specs=(
            P("dp", "tensor", None),
            P("dp", "tensor", None),
            P("dp"),
            P("dp"),
            P("dp", None, "tensor"),
            P("tensor", "dp"),
            P("dp", None, "tensor"),
            P("tensor", "dp"),
        ),
        check_vma=False,
    )
```

profile of v0, /device:TPU:0, one launch (start us, length us, event | category | flops | bytes accessed | tf_op | source)
XLA Modules:
  0.0 944.2 jit_solution(6730951717546695902)
XLA Ops:
  11.7 6.0 all-gather
  19.1 6.3 all_gather.33
  26.5 9.2 all_gather.32
  35.6 57.8 %all-gather.8.cloned.1.call-done = bf16[2048,1024]{1,0:T(8,128)(2,1)} async-done(((bf16[256,1024]{1,0:T(8,128)(2,1)}), bf16[2048,1024]{1,0:T(8,128)(2,1)}) %all-gather.8.cloned.1.call-update) | async-done | bytes 4194320 | tf_op jit(solution)/shard_map/all_gather | solution.py:196
  93.5 4.2 fusion.68
  100.9 22.1 %while.26 = (s32[]{:T(128)}, bf16[4,512,2,64]{1,3,2,0:T(8,128)(2,1)S(1)}, f32[4,2,512]{2,1,0:T(2,128)S(1)}, s32[4]{0:T(128)S(1)}, bf16[2176,2,64]{0,2,1:T(8,128)...) while((s32[]{:T(128)}, ...), condition=%wide.region_5.6_spmd, body=%wide.region_2.5_spmd.sunk | while | flops 176684544 | bytes 9815796 | solution.py:104
  128.3 5.1 all-gather.1
  133.3 81.3 %reduce-scatter.12.cloned.1.call-done = bf16[256,1024]{1,0:T(8,128)(2,1)} async-done(((bf16[2048,1024]{1,0:T(8,128)(2,1)}), bf16[256,1024]{1,0:T(8,128)(2,1)}) %reduce-scatter.12.cloned.1.call-update) | async-done | bytes 524304 | tf_op jit(solution)/shard_map/reduce_scatter | solution.py:206
  219.4 8.4 all_gather.37
  227.8 61.6 %all-gather.10.cloned.1.call-done = bf16[2048,1024]{1,0:T(8,128)(2,1)} async-done(((bf16[256,1024]{1,0:T(8,128)(2,1)}), bf16[2048,1024]{1,0:T(8,128)(2,1)}) %all-gather.10.cloned.1.call-update) | async-done | bytes 4194320 | tf_op jit(solution)/shard_map/all_gather | solution.py:214
  289.5 7.9 fusion.74
  297.4 65.8 %all-gather.14.cloned.1.call-done = bf16[2048,1024]{1,0:T(8,128)(2,1)} async-done(((bf16[256,1024]{1,0:T(8,128)(2,1)}), bf16[2048,1024]{1,0:T(8,128)(2,1)}) %all-gather.14.cloned.1.call-update) | async-done | bytes 4194320 | tf_op jit(solution)/shard_map/all_gather | solution.py:228
  363.2 6.9 fusion.80
  371.6 5.1 bitcast_convert_fusion
  380.9 4.4 convolution_convert_fusion.1
  385.3 78.5 %reduce-scatter.16.cloned.1.call-done = bf16[256,1024]{1,0:T(8,128)(2,1)} async-done(((bf16[2048,1024]{1,0:T(8,128)(2,1)}), bf16[256,1024]{1,0:T(8,128)(2,1)}) %reduce-scatter.16.cloned.1.call-update) | async-done | bytes 524304 | tf_op jit(solution)/shard_map/reduce_scatter | solution.py:237
  465.3 89.9 %reduce-scatter.14.cloned.1.call-done = bf16[256,1024]{1,0:T(8,128)(2,1)} async-done(((bf16[2048,1024]{1,0:T(8,128)(2,1)}), bf16[256,1024]{1,0:T(8,128)(2,1)}) %reduce-scatter.14.cloned.1.call-update) | async-done | bytes 524304 | tf_op jit(solution)/shard_map/reduce_scatter | solution.py:220
  558.5 5.1 convolution_convert_fusion.4
  563.9 7.0 fusion.83
  570.9 59.8 %all-gather.16.cloned.1.call-done = bf16[2048,1024]{1,0:T(8,128)(2,1)} async-done(((bf16[256,1024]{1,0:T(8,128)(2,1)}), bf16[2048,1024]{1,0:T(8,128)(2,1)}) %all-gather.16.cloned.1.call-update) | async-done | bytes 4194320 | tf_op jit(solution)/shard_map/all_gather | solution.py:248
  630.8 4.5 convolution_convert_fusion.3
  637.5 105.5 %while.27 = (s32[]{:T(128)}, f32[2176,2,64]{0,2,1:T(8,128)}, f32[2176,2,64]{0,2,1:T(8,128)}, f32[4,512,2,64]{1,0,3,2:T(4,128)}, s32[4]{0:T(128)S(1)}, /*index=5*...) while((s32[]{:T(128)}, f32[2176,2,64]{0,2,1:T(8,128)}, ...), condition=%wide.region_15.16_spmd, body=%wide.region_13.15_spmd.sunk | while | flops 430411520 | bytes 33158988 | solution.py:156
  651.5 6.1 dynamic_update_slice.31
  672.6 4.2 fusion.178
  678.0 6.1 dynamic_update_slice.31
  704.4 6.1 dynamic_update_slice.31
  730.6 6.1 dynamic_update_slice.31
  762.4 5.7 convolution_convert_fusion
  776.0 24.1 %reduce-scatter.20.cloned.1.call-done = bf16[256,3,128]{2,0,1:T(8,128)(2,1)} async-done(((bf16[1024,3,128]{2,0,1:T(8,128)(2,1)}), bf16[256,3,128]{2,0,1:T(8,128)(2,1)}) %reduce-scatter.20.cloned.1.call-update) | async-done | bytes 196624 | tf_op jit(solution)/shard_map/reduce_scatter | solution.py:281
  801.8 90.0 %reduce-scatter.18.cloned.1.call-done = bf16[256,1024]{1,0:T(8,128)(2,1)} async-done(((bf16[2048,1024]{1,0:T(8,128)(2,1)}), bf16[256,1024]{1,0:T(8,128)(2,1)}) %reduce-scatter.18.cloned.1.call-update) | async-done | bytes 524304 | tf_op jit(solution)/shard_map/reduce_scatter | solution.py:271
  896.7 17.3 %reduce-scatter.28.cloned.1.call-done = bf16[256,2]{1,0:T(8,128)(2,1)} async-done(((bf16[1024,2]{1,0:T(8,128)(2,1)}), bf16[256,2]{1,0:T(8,128)(2,1)}) %reduce-scatter.28.cloned.1.call-update) | async-done | bytes 1040
  914.9 21.4 %psum.7 = f32[2,256]{1,0:T(2,128)S(1)} all-reduce(bf16[2,256]{1,0:T(2,128)(2,1)S(1)} %copy.35), channel_id=1, replica_groups=mesh['dp'=4,'tensor'=8] {'tensor'}, use_global_device_ids=true, to_apply=%region_22.23 | all-reduce | flops 512 | bytes 3072 | tf_op jit(solution)/shard_map/psum | solution.py:303
  (234 shorter events, 152.8 us)
Async XLA Ops:
  8.0 9.7 %copy-start = (f32[1,256,1024]{2,1,0:T(8,128)S(1)}, f32[1,256,1024]{2,1,0:T(8,128)}, u32[]{:S(2)}) copy-start(f32[1,256,1024]{2,1,0:T(8,128)} %param.14) | copy-start | bytes 3145732
  8.0 10.8 %copy-start.15 = (bf16[256,3,128]{2,0,1:T(8,128)(2,1)S(1)}, bf16[256,3,128]{2,0,1:T(8,128)(2,1)}, u32[]{:S(2)}) copy-start(bf16[256,3,128]{2,0,1:T(8,128)(2,1)} %param.19) | copy-start | bytes 589828
  8.0 11.0 %copy-start.19 = (s32[1,2048]{1,0:T(1,128)S(1)}, s32[1,2048]{1,0:T(1,128)}, u32[]{:S(2)}) copy-start(s32[1,2048]{1,0:T(1,128)} %param.16) | copy-start | bytes 24580
  8.0 11.0 %copy-start.17 = (s32[1,2048]{1,0:T(1,128)S(1)}, s32[1,2048]{1,0:T(1,128)}, u32[]{:S(2)}) copy-start(s32[1,2048]{1,0:T(1,128)} %param.15) | copy-start | bytes 24580
  8.0 11.1 %copy-start.18 = (bf16[128,256]{1,0:T(8,128)(2,1)S(1)}, bf16[128,256]{1,0:T(8,128)(2,1)}, u32[]{:S(2)}) copy-start(bf16[128,256]{1,0:T(8,128)(2,1)} %param.20) | copy-start | bytes 196612
  8.1 85.4 %all-gather.8.cloned.1.call-start = ((), (), s32[]{:S(2)}) async-start(), calls=%async_computation.9 | async-start | bytes 4718592 | tf_op jit(solution)/shard_map/all_gather | solution.py:196
  18.8 195.9 %reduce-scatter.12.cloned.1.call-start = ((), (), s32[]{:S(2)}) async-start(), calls=%async_computation.10 | async-start | bytes 4718592 | tf_op jit(solution)/shard_map/reduce_scatter | solution.py:206
  26.5 71.7 %copy-start.4 = (f32[2048,64]{0,1:T(8,128)}, f32[2048,64]{0,1:T(8,128)S(1)}, u32[]{:S(2)}) copy-start(f32[2048,64]{0,1:T(8,128)S(1)} %get-tuple-element.205) | copy-start | bytes 1572868
  123.0 4.6 copy-start.9
  127.6 100.2 %all-gather.12.cloned.1.call-start = ((), (), s32[]{:S(2)}) async-start(), calls=%async_computation.12 | async-start | bytes 1679360 | tf_op jit(solution)/shard_map/all_gather | solution.py:184
  128.2 161.3 %all-gather.10.cloned.1.call-start = ((), (), s32[]{:S(2)}) async-start(), calls=%async_computation.11 | async-start | bytes 4718592 | tf_op jit(solution)/shard_map/all_gather | solution.py:214
  215.9 3.5 copy-start.16
  217.2 146.0 %all-gather.14.cloned.1.call-start = ((), (), s32[]{:S(2)}) async-start(), calls=%async_computation.14 | async-start | bytes 4718592 | tf_op jit(solution)/shard_map/all_gather | solution.py:228
  219.3 244.4 %reduce-scatter.16.cloned.1.call-start = ((), (), s32[]{:S(2)}) async-start(), calls=%async_computation.15 | async-start | bytes 4718592 | tf_op jit(solution)/shard_map/reduce_scatter | solution.py:237
  363.2 8.4 copy-start.21
  376.7 178.5 %reduce-scatter.14.cloned.1.call-start = ((), (), s32[]{:S(2)}) async-start(), calls=%async_computation.13 | async-start | bytes 4718592 | tf_op jit(solution)/shard_map/reduce_scatter | solution.py:220
  385.3 170.0 %copy-start.8 = (f32[1,256,1024]{2,1,0:T(8,128)S(1)}, f32[1,256,1024]{2,1,0:T(8,128)}, u32[]{:S(2)}) copy-start(f32[1,256,1024]{2,1,0:T(8,128)} %param.23) | copy-start | bytes 3145732
  385.3 245.5 %all-gather.16.cloned.1.call-start = ((), (), s32[]{:S(2)}) async-start(), calls=%async_computation.16 | async-start | bytes 4718592 | tf_op jit(solution)/shard_map/all_gather | solution.py:248
  558.5 5.4 copy-start.24
  558.5 209.8 %reduce-scatter.26.cloned.1.call-start = ((), (), s32[]{:S(2)}) async-start(), calls=%async_computation.21 | async-start | bytes 839680 | tf_op jit(solution)/shard_map/reduce_scatter | solution.py:296
  563.6 206.4 %reduce-scatter.24.cloned.1.call-start = ((), (), s32[]{:S(2)}) async-start(), calls=%async_computation.20 | async-start | bytes 1679360 | tf_op jit(solution)/shard_map/reduce_scatter | solution.py:287
  570.9 203.6 %reduce-scatter.22.cloned.1.call-start = ((), (), s32[]{:S(2)}) async-start(), calls=%async_computation.19 | async-start | bytes 327680 | tf_op jit(solution)/shard_map/reduce_scatter | solution.py:293
  743.0 3.9 copy-start.7
  746.8 3.7 copy-start.2
  746.8 3.7 copy-start.5
  755.9 44.1 %reduce-scatter.20.cloned.1.call-start = ((), (), s32[]{:S(2)}) async-start(), calls=%async_computation.18 | async-start | bytes 983040 | tf_op jit(solution)/shard_map/reduce_scatter | solution.py:281
  756.2 2.9 copy-start.20
  759.0 3.3 copy-start.13
  762.3 129.5 %reduce-scatter.18.cloned.1.call-start = ((), (), s32[]{:S(2)}) async-start(), calls=%async_computation.17 | async-start | bytes 4718592 | tf_op jit(solution)/shard_map/reduce_scatter | solution.py:271
  768.1 123.7 %copy-start.1 = (f32[1,256,1024]{2,1,0:T(8,128)S(1)}, f32[1,256,1024]{2,1,0:T(8,128)}, u32[]{:S(2)}) copy-start(f32[1,256,1024]{2,1,0:T(8,128)} %param.14) | copy-start | bytes 3145732
  768.2 126.1 %copy-start.6 = (f32[256,1024]{1,0:T(8,128)S(1)}, f32[256,1024]{1,0:T(8,128)}, u32[]{:S(2)}) copy-start(f32[256,1024]{1,0:T(8,128)} %get-tuple-element.176) | copy-start | bytes 3145732
  768.2 145.8 %reduce-scatter.28.cloned.1.call-start = ((), (), s32[]{:S(2)}) async-start(), calls=%async_computation.22 | async-start | bytes 327680
  (8 other events, 10.9 us)
Sparse Core Ops, SparseCore 0:
  18.9 74.5 all-gather.7
  127.7 86.8 reduce-scatter.11
  376.9 86.8 reduce-scatter.15
  467.3 87.9 reduce-scatter.13
Sparse Core Ops, SparseCore 1:
  129.6 16.9 all-gather.11
  217.3 72.1 all-gather.9
  292.0 71.1 all-gather.13
  558.5 72.2 all-gather.15
  633.9 21.1 reduce-scatter.25
  657.6 26.5 reduce-scatter.23
  756.0 18.4 reduce-scatter.21
  776.9 23.1 reduce-scatter.19
  803.6 88.2 reduce-scatter.17
  894.4 19.6 reduce-scatter.27
where the time goes:
time: 954 us; the launch traced here: 944 us
  waiting for transfers between devices  630 us (66%)
  matrix products  133 us (14%)
  blocking collectives  56.3 us (6%)
  local copies, waits for them, and re-layouts  52.7 us (6%)
  other arithmetic  42.4 us (4%)
  between operations  16.1 us (2%)
  loops' own time  13.3 us (1%)
    reduce_scatter x1, waiting for transfers between devices, body(): lax.psum_scatter(jnp.dot(grad_proj, qkv_matrix.T, preferred_element_type=...  90 us
    reduce_scatter x1, waiting for transfers between devices, body(): lax.psum_scatter(jnp.dot(hidden, contract_full, preferred_element_type=jn...  89.9 us
    reduce_scatter x1, waiting for transfers between devices, body(): lax.psum_scatter(jnp.dot(context_rows, output_full, preferred_element_typ...  81.3 us
    reduce_scatter x1, waiting for transfers between devices, body(): lax.psum_scatter(jnp.dot(grad_units, expand_matrix.T, preferred_element_t...  78.5 us
    all_gather x1, waiting for transfers between devices, body(): lax.all_gather(upstream.astype(jnp.bfloat16), 'tensor', axis=0, tiled=True)  65.8 us
    all_gather x1, waiting for transfers between devices, body(): rows_two = lax.all_gather(rounded_two, 'tensor', axis=0, tiled=True)  61.6 us
    all_gather x1, waiting for transfers between devices, body(): lax.all_gather(grad_mid.astype(jnp.bfloat16), 'tensor', axis=0, tiled=True)  59.8 us
    all_gather x1, waiting for transfers between devices, body(): rows_one = lax.all_gather(rounded_one, 'tensor', axis=0, tiled=True)  57.8 us
  transfers between devices with their start and end apart: 14, of which 11 were waited for; matrix products, arithmetic and copies ran while one was open for 18% of the time, Pallas kernels for 0%

commit v1 on v0

--- a/solution.py
+++ b/solution.py
@@ -245,7 +245,16 @@
     through_two, gain_part = norm_backward(grad_two, normed_two, inverse_two, second_gain)
     gain_second = gain_part
     grad_mid = upstream + through_two
-    rows_mid = lax.all_gather(grad_mid.astype(jnp.bfloat16), "tensor", axis=0, tiled=True)
+    shard = grad_mid.astype(jnp.bfloat16)
+    ways, here = (lax.axis_size("tensor"), lax.axis_index("tensor"))
+    grown, reach_2 = (shard, 1)
+    while reach_2 < ways:
+        theirs = lax.ppermute(grown, "tensor", [(d, d ^ reach_2) for d in range(ways)])
+        mine_first = jnp.concatenate([grown, theirs], axis=0)
+        theirs_first = jnp.concatenate([theirs, grown], axis=0)
+        grown = jnp.where(here & reach_2 == 0, mine_first, theirs_first)
+        reach_2 = 2 * reach_2
+    rows_mid = grown
     grad_output = jnp.dot(context_rows.T, rows_mid, preferred_element_type=jnp.float32)
     grad_context = (
         jnp.dot(rows_mid, output_full.T, preferred_element_type=jnp.float32)

time: 954 us -> 1020 us (1.069)
  waiting for transfers between devices: 630 us -> 671 us
    ppermute x0 -> x3, waiting for transfers between devices: none -> 111 us  [body(): lax.ppermute(grown, 'tensor', [(d, d ^ reach_2) for d in range(ways)])]
    all_gather x1 -> x0, waiting for transfers between devices: 59.8 us -> none  [body(): lax.all_gather(grad_mid.astype(jnp.bfloat16), 'tensor', axis=0, tiled=True)]
    all_gather x1, blocking collectives: 8.41 us -> 19.1 us  [body(): lax.all_gather(contract_weight, 'dp', axis=1, tiled=True)]
    all_gather x1, waiting for transfers between devices: 61.6 us -> 51 us  [body(): rows_two = lax.all_gather(rounded_two, 'tensor', axis=0, tiled=True)]
  transfers between devices with their start and end apart: 14 -> 16, of which waited for: 11 -> 13; matrix products, arithmetic and copies ran while one was open for 18% -> 17% of each run, Pallas kernels for 0% -> 0%
where the time goes in v1:
time: 1020 us; the launch traced here: 1010 us
  waiting for transfers between devices  671 us (66%)
  matrix products  137 us (13%)
  blocking collectives  66.4 us (7%)
  local copies, waits for them, and re-layouts  55.7 us (5%)
  other arithmetic  46.6 us (5%)
  between operations  16.6 us (2%)
  loops' own time  13.2 us (1%)
    ppermute x3, waiting for transfers between devices, body(): lax.ppermute(grown, 'tensor', [(d, d ^ reach_2) for d in range(ways)])  111 us
    reduce_scatter x1, waiting for transfers between devices, body(): lax.psum_scatter(jnp.dot(grad_proj, qkv_matrix.T, preferred_element_type=...  90 us
    reduce_scatter x1, waiting for transfers between devices, body(): lax.psum_scatter(jnp.dot(hidden, contract_full, preferred_element_type=jn...  89.9 us
    reduce_scatter x1, waiting for transfers between devices, body(): lax.psum_scatter(jnp.dot(context_rows, output_full, preferred_element_typ...  81.3 us
    reduce_scatter x1, waiting for transfers between devices, body(): lax.psum_scatter(jnp.dot(grad_units, expand_matrix.T, preferred_element_t...  78.4 us
    all_gather x1, waiting for transfers between devices, body(): lax.all_gather(upstream.astype(jnp.bfloat16), 'tensor', axis=0, tiled=True)  65.8 us
    all_gather x1, waiting for transfers between devices, body(): rows_one = lax.all_gather(rounded_one, 'tensor', axis=0, tiled=True)  58.3 us
    all_gather x1, waiting for transfers between devices, body(): rows_two = lax.all_gather(rounded_two, 'tensor', axis=0, tiled=True)  51 us
  transfers between devices with their start and end apart: 16, of which 13 were waited for; matrix products, arithmetic and copies ran while one was open for 17% of the time, Pallas kernels for 0%

profile of v1, /device:TPU:0, one launch (start us, length us, event | category | flops | bytes accessed | tf_op | source)
XLA Modules:
  0.0 1013.9 jit_solution(69204000788837644)
XLA Ops:
  11.7 6.0 all-gather
  19.1 6.3 all_gather.30
  26.5 8.7 all_gather.29
  35.2 58.3 %all-gather.7.cloned.1.call-done = bf16[2048,1024]{1,0:T(8,128)(2,1)} async-done(((bf16[256,1024]{1,0:T(8,128)(2,1)}), bf16[2048,1024]{1,0:T(8,128)(2,1)}) %all-gather.7.cloned.1.call-update) | async-done | bytes 4194320 | tf_op jit(solution)/shard_map/all_gather | solution.py:196
  99.8 24.3 %while.26 = (s32[]{:T(128)}, bf16[4,512,2,64]{1,3,2,0:T(8,128)(2,1)}, f32[4,2,512]{2,1,0:T(2,128)S(1)}, s32[4]{0:T(128)S(1)}, bf16[2176,2,64]{0,2,1:T(8,128)(2,1...) while((s32[]{:T(128)}, ...), condition=%wide.region_5.6_spmd, body=%wide.region_2.5_spmd.sunk | while | flops 176684544 | bytes 9816304 | solution.py:104
  130.8 5.1 all-gather.1
  135.9 81.3 %reduce-scatter.12.cloned.1.call-done = bf16[256,1024]{1,0:T(8,128)(2,1)} async-done(((bf16[2048,1024]{1,0:T(8,128)(2,1)}), bf16[256,1024]{1,0:T(8,128)(2,1)}) %reduce-scatter.12.cloned.1.call-update) | async-done | bytes 524304 | tf_op jit(solution)/shard_map/reduce_scatter | solution.py:206
  221.9 19.1 %all_gather.34 = bf16[328,1024]{1,0:T(8,128)(2,1)S(1)} all-gather(bf16[328,256]{1,0:T(8,128)(2,1)S(1)} %copy-done.19), channel_id=1, replica_groups=mesh['dp'=4,'tensor'=8] {'dp'}, dimensions={1}, use_global_device_ids=true | all-gather | bytes 839680 | tf_op jit(solution)/shard_map/all_gather | solution.py:186
  241.0 51.0 %all-gather.9.cloned.1.call-done = bf16[2048,1024]{1,0:T(8,128)(2,1)} async-done(((bf16[256,1024]{1,0:T(8,128)(2,1)}), bf16[2048,1024]{1,0:T(8,128)(2,1)}) %all-gather.9.cloned.1.call-update) | async-done | bytes 4194320 | tf_op jit(solution)/shard_map/all_gather | solution.py:214
  292.0 8.0 fusion.74
  299.9 65.8 %all-gather.13.cloned.1.call-done = bf16[2048,1024]{1,0:T(8,128)(2,1)} async-done(((bf16[256,1024]{1,0:T(8,128)(2,1)}), bf16[2048,1024]{1,0:T(8,128)(2,1)}) %all-gather.13.cloned.1.call-update) | async-done | bytes 4194320 | tf_op jit(solution)/shard_map/all_gather | solution.py:228
  365.7 6.9 fusion.80
  374.1 5.1 bitcast_convert_fusion
  387.9 78.4 %reduce-scatter.16.cloned.1.call-done = bf16[256,1024]{1,0:T(8,128)(2,1)} async-done(((bf16[2048,1024]{1,0:T(8,128)(2,1)}), bf16[256,1024]{1,0:T(8,128)(2,1)}) %reduce-scatter.16.cloned.1.call-update) | async-done | bytes 524304 | tf_op jit(solution)/shard_map/reduce_scatter | solution.py:237
  467.9 89.9 %reduce-scatter.14.cloned.1.call-done = bf16[256,1024]{1,0:T(8,128)(2,1)} async-done(((bf16[2048,1024]{1,0:T(8,128)(2,1)}), bf16[256,1024]{1,0:T(8,128)(2,1)}) %reduce-scatter.14.cloned.1.call-update) | async-done | bytes 524304 | tf_op jit(solution)/shard_map/reduce_scatter | solution.py:220
  562.1 11.8 %collective-permute-done = bf16[256,1024]{1,0:T(8,128)(2,1)S(1)} collective-permute-done((bf16[256,1024]{1,0:T(8,128)(2,1)S(1)}, bf16[256,1024]{1,0:T(8,128)(2,1)S(1)}, u32[]{:S(2)}, u32[]{:S(2)}) %collective-permute-start) | collective-permute-done | bytes 524320 | tf_op jit(solution)/shard_map/ppermute | solution.py:252
  576.2 22.1 %collective-permute-done.1 = bf16[512,1024]{1,0:T(8,128)(2,1)} collective-permute-done((bf16[512,1024]{1,0:T(8,128)(2,1)S(1)}, bf16[512,1024]{1,0:T(8,128)(2,1)}, u32[]{:S(2)}, u32[]{:S(2)}) %collective-permute-start.1) | collective-permute-done | bytes 1048608 | tf_op jit(solution)/shard_map/ppermute | solution.py:252
  604.9 4.6 convolution_convert_fusion.4
  609.6 7.0 fusion.83
  616.8 77.2 %collective-permute-done.2 = bf16[1024,1024]{1,0:T(8,128)(2,1)} collective-permute-done((bf16[1024,1024]{1,0:T(8,128)(2,1)}, bf16[1024,1024]{1,0:T(8,128)(2,1)}, u32[]{:S(2)}, u32[]{:S(2)}) %collective-permute-start.2) | collective-permute-done | bytes 2097184 | tf_op jit(solution)/shard_map/ppermute | solution.py:252
  694.0 5.4 convolution_convert_fusion.3
  701.6 105.4 %while.27 = (s32[]{:T(128)}, f32[2176,2,64]{0,2,1:T(8,128)}, f32[2176,2,64]{0,2,1:T(8,128)}, f32[4,512,2,64]{1,0,3,2:T(4,128)}, s32[4]{0:T(128)S(1)}, /*index=5*...) while((s32[]{:T(128)}, f32[2176,2,64]{0,2,1:T(8,128)}, ...), condition=%wide.region_15.16_spmd, body=%wide.region_13.15_spmd.sunk | while | flops 430411520 | bytes 33158988 | solution.py:156
  715.6 6.1 dynamic_update_slice.31
  741.9 6.1 dynamic_update_slice.31
  768.3 6.1 dynamic_update_slice.31
  794.6 6.1 dynamic_update_slice.31
  817.1 5.4 convolution_convert_fusion.5
  830.7 5.8 convolution_convert_fusion
  845.3 24.1 %reduce-scatter.20.cloned.1.call-done = bf16[256,3,128]{2,0,1:T(8,128)(2,1)} async-done(((bf16[1024,3,128]{2,0,1:T(8,128)(2,1)}), bf16[256,3,128]{2,0,1:T(8,128)(2,1)}) %reduce-scatter.20.cloned.1.call-update) | async-done | bytes 196624 | tf_op jit(solution)/shard_map/reduce_scatter | solution.py:290
  871.1 90.0 %reduce-scatter.18.cloned.1.call-done = bf16[256,1024]{1,0:T(8,128)(2,1)} async-done(((bf16[2048,1024]{1,0:T(8,128)(2,1)}), bf16[256,1024]{1,0:T(8,128)(2,1)}) %reduce-scatter.18.cloned.1.call-update) | async-done | bytes 524304 | tf_op jit(solution)/shard_map/reduce_scatter | solution.py:280
  966.0 17.3 %reduce-scatter.28.cloned.1.call-done = bf16[256,2]{1,0:T(8,128)(2,1)} async-done(((bf16[1024,2]{1,0:T(8,128)(2,1)}), bf16[256,2]{1,0:T(8,128)(2,1)}) %reduce-scatter.28.cloned.1.call-update) | async-done | bytes 1040
  984.2 21.3 %psum.7 = f32[2,256]{1,0:T(2,128)S(1)} all-reduce(bf16[2,256]{1,0:T(2,128)(2,1)S(1)} %copy.35), channel_id=1, replica_groups=mesh['dp'=4,'tensor'=8] {'tensor'}, use_global_device_ids=true, to_apply=%region_22.23 | all-reduce | flops 512 | bytes 3072 | tf_op jit(solution)/shard_map/psum | solution.py:312
  (243 shorter events, 177.9 us)
Async XLA Ops:
  8.0 9.7 copy-start
  8.0 10.8 %copy-start.18 = (bf16[256,3,128]{2,0,1:T(8,128)(2,1)S(1)}, bf16[256,3,128]{2,0,1:T(8,128)(2,1)}, u32[]{:S(2)}) copy-start(bf16[256,3,128]{2,0,1:T(8,128)(2,1)} %param.19) | copy-start | bytes 589828
  8.0 11.0 %copy-start.22 = (s32[1,2048]{1,0:T(1,128)S(1)}, s32[1,2048]{1,0:T(1,128)}, u32[]{:S(2)}) copy-start(s32[1,2048]{1,0:T(1,128)} %param.16) | copy-start | bytes 24580
  8.0 11.0 %copy-start.20 = (s32[1,2048]{1,0:T(1,128)S(1)}, s32[1,2048]{1,0:T(1,128)}, u32[]{:S(2)}) copy-start(s32[1,2048]{1,0:T(1,128)} %param.15) | copy-start | bytes 24580
  8.0 11.1 %copy-start.21 = (bf16[128,256]{1,0:T(8,128)(2,1)S(1)}, bf16[128,256]{1,0:T(8,128)(2,1)}, u32[]{:S(2)}) copy-start(bf16[128,256]{1,0:T(8,128)(2,1)} %param.20) | copy-start | bytes 196612
  8.1 85.4 %all-gather.7.cloned.1.call-start = ((), (), s32[]{:S(2)}) async-start(), calls=%async_computation.9 | async-start | bytes 4718592 | tf_op jit(solution)/shard_map/all_gather | solution.py:196
  18.8 198.4 %reduce-scatter.12.cloned.1.call-start = ((), (), s32[]{:S(2)}) async-start(), calls=%async_computation.10 | async-start | bytes 4718592 | tf_op jit(solution)/shard_map/reduce_scatter | solution.py:206
  26.5 71.5 %copy-start.3 = (f32[2048,64]{0,1:T(8,128)}, f32[2048,64]{0,1:T(8,128)S(1)}, u32[]{:S(2)}) copy-start(f32[2048,64]{0,1:T(8,128)S(1)} %get-tuple-element.205) | copy-start | bytes 1572868
  35.2 62.3 %copy-start.15 = (bf16[1024,3,128]{0,2,1:T(8,128)(2,1)}, bf16[1024,3,128]{0,2,1:T(8,128)(2,1)S(1)}, u32[]{:S(2)}) copy-start(bf16[1024,3,128]{0,2,1:T(8,128)(2,1)S(1)} %all_gather.29) | copy-start | bytes 2359300
  124.1 6.0 copy-start.9
  124.1 6.0 copy-start.17
  130.1 110.8 %all-gather.11.cloned.1.call-start = ((), (), s32[]{:S(2)}) async-start(), calls=%async_computation.12 | async-start | bytes 1679360 | tf_op jit(solution)/shard_map/all_gather | solution.py:184
  130.7 161.2 %all-gather.9.cloned.1.call-start = ((), (), s32[]{:S(2)}) async-start(), calls=%async_computation.11 | async-start | bytes 4718592 | tf_op jit(solution)/shard_map/all_gather | solution.py:214
  219.7 146.0 %all-gather.13.cloned.1.call-start = ((), (), s32[]{:S(2)}) async-start(), calls=%async_computation.14 | async-start | bytes 4718592 | tf_op jit(solution)/shard_map/all_gather | solution.py:228
  221.8 244.5 %reduce-scatter.16.cloned.1.call-start = ((), (), s32[]{:S(2)}) async-start(), calls=%async_computation.15 | async-start | bytes 4718592 | tf_op jit(solution)/shard_map/reduce_scatter | solution.py:237
  365.7 8.4 copy-start.24
  379.3 178.5 %reduce-scatter.14.cloned.1.call-start = ((), (), s32[]{:S(2)}) async-start(), calls=%async_computation.13 | async-start | bytes 4718592 | tf_op jit(solution)/shard_map/reduce_scatter | solution.py:220
  387.8 170.0 %copy-start.8 = (f32[1,256,1024]{2,1,0:T(8,128)S(1)}, f32[1,256,1024]{2,1,0:T(8,128)}, u32[]{:S(2)}) copy-start(f32[1,256,1024]{2,1,0:T(8,128)} %param.23) | copy-start | bytes 3145732
  387.8 448.7 %reduce-scatter.26.cloned.1.call-start = ((), (), s32[]{:S(2)}) async-start(), calls=%async_computation.20 | async-start | bytes 839680 | tf_op jit(solution)/shard_map/reduce_scatter | solution.py:305
  560.6 13.3 %collective-permute-start = (bf16[256,1024]{1,0:T(8,128)(2,1)S(1)}, bf16[256,1024]{1,0:T(8,128)(2,1)S(1)}, u32[]{:S(2)}, u32[]{:S(2)}) collective-permute-start(bf16[256,1024]{1,0:T(8,128)(2,1)S(1)} %get-tuple-element.175), channel_id=1, source_target_pairs={{0,1},{1,0},{2,3},{3,2},{4,5},{5,4},{6,7},{7,6},{8,9},{9,8},{10,11... | collective-permute-start | bytes 1572872 | tf_op jit(solution)/shard_map/ppermute | solution.py:252
  574.4 30.5 %copy-start.14 = (bf16[2048,328]{0,1:T(8,128)(2,1)S(1)}, bf16[2048,328]{0,1:T(8,128)(2,1)}, u32[]{:S(2)}) copy-start(bf16[2048,328]{0,1:T(8,128)(2,1)} %copy-done.13) | copy-start | bytes 4030468
  574.4 23.8 %collective-permute-start.1 = (bf16[512,1024]{1,0:T(8,128)(2,1)S(1)}, bf16[512,1024]{1,0:T(8,128)(2,1)}, u32[]{:S(2)}, u32[]{:S(2)}) collective-permute-start(bf16[512,1024]{1,0:T(8,128)(2,1)S(1)} %maximum_select_fusion.2), channel_id=1, source_target_pairs={{0,2},{1,3},{2,0},{3,1},{4,6},{5,7},{6,4},{7,5},{8,10},{9,11},{10,... | collective-permute-start | bytes 3145736 | tf_op jit(solution)/shard_map/ppermute | solution.py:252
  602.2 91.8 %collective-permute-start.2 = (bf16[1024,1024]{1,0:T(8,128)(2,1)}, bf16[1024,1024]{1,0:T(8,128)(2,1)}, u32[]{:S(2)}, u32[]{:S(2)}) collective-permute-start(bf16[1024,1024]{1,0:T(8,128)(2,1)} %maximum_select_fusion.1), channel_id=1, source_target_pairs={{0,4},{1,5},{2,6},{3,7},{4,0},{5,1},{6,2},{7,3},{8,12},{9,13},{10,... | collective-permute-start | bytes 6291464 | tf_op jit(solution)/shard_map/ppermute | solution.py:252
  609.5 228.8 %reduce-scatter.24.cloned.1.call-start = ((), (), s32[]{:S(2)}) async-start(), calls=%async_computation.19 | async-start | bytes 1679360 | tf_op jit(solution)/shard_map/reduce_scatter | solution.py:296
  616.6 227.1 %reduce-scatter.22.cloned.1.call-start = ((), (), s32[]{:S(2)}) async-start(), calls=%async_computation.18 | async-start | bytes 327680 | tf_op jit(solution)/shard_map/reduce_scatter | solution.py:302
  806.9 5.0 copy-start.2
  806.9 5.0 copy-start.4
  822.6 46.8 %reduce-scatter.20.cloned.1.call-start = ((), (), s32[]{:S(2)}) async-start(), calls=%async_computation.17 | async-start | bytes 983040 | tf_op jit(solution)/shard_map/reduce_scatter | solution.py:290
  830.3 130.7 %reduce-scatter.18.cloned.1.call-start = ((), (), s32[]{:S(2)}) async-start(), calls=%async_computation.16 | async-start | bytes 4718592 | tf_op jit(solution)/shard_map/reduce_scatter | solution.py:280
  836.4 124.6 %copy-start.1 = (f32[1,256,1024]{2,1,0:T(8,128)S(1)}, f32[1,256,1024]{2,1,0:T(8,128)}, u32[]{:S(2)}) copy-start(f32[1,256,1024]{2,1,0:T(8,128)} %param.14) | copy-start | bytes 3145732
  836.5 127.1 %copy-start.7 = (f32[256,1024]{1,0:T(8,128)S(1)}, f32[256,1024]{1,0:T(8,128)}, u32[]{:S(2)}) copy-start(f32[256,1024]{1,0:T(8,128)} %get-tuple-element.176) | copy-start | bytes 3145732
  836.5 146.8 %reduce-scatter.28.cloned.1.call-start = ((), (), s32[]{:S(2)}) async-start(), calls=%async_computation.21 | async-start | bytes 327680
  (12 other events, 23.2 us)
Sparse Core Ops, SparseCore 0:
  18.9 74.5 all-gather.6
  130.2 86.8 reduce-scatter.11
  379.4 86.8 reduce-scatter.15
  469.8 87.9 reduce-scatter.13
Sparse Core Ops, SparseCore 1:
  132.2 16.9 all-gather.10
  219.8 72.1 all-gather.8
  294.5 71.1 all-gather.12
  609.6 21.3 reduce-scatter.25
  633.6 26.6 reduce-scatter.23
  822.7 21.0 reduce-scatter.21
  846.2 23.1 reduce-scatter.19
  872.8 88.2 reduce-scatter.17
  963.6 19.6 reduce-scatter.27
